TPU v7x, 256 devices: a whole 4x4x8 slice. The times are simulated.
256 devices in a mesh: freq: 32 (over x, y, core), mode: 8 (over z).
Axes of the slice: x: 4, y: 4, z: 8, core: 2. Of those that a mesh axis runs over, the one named last changes fastest.
Arguments:
- excitation: bfloat16 [16, 2, 1024, 2048], P(None, None, 'freq', 'mode'), may hold values from -6 to 6
- coupling: bfloat16 [3, 32, 2, 2048, 2048], P(None, 'freq', None, 'mode'), may hold values from -3 to 3, as said below
- wavenumber: float32 [1024, 2048], P('freq', 'mode'), may hold values from 0.02 to 0.2
- mode_counts: int32 [1024], P('freq'), may hold values from 128 to 2048, as said below
- seg_steps: int32 [3], replicated, may hold values from 8 to 64
- shapes: bfloat16 [32, 2048, 512], P('freq'), may hold values from -0.125 to 0.125
- spectrum: float32 [2, 1024], P(None, 'freq'), may hold values from -6 to 6
Outputs:
- traces: float32 [16, 512, 4096], P('mode', 'freq')
Inputs may be any that keep to these rules, and one draw needn't show every extreme that they name: `mode_counts`: each count is a multiple of 128; counts tend to rise with frequency; the first frequency has 128 modes and the last has all 2048. `coupling`: the real part of each matrix is near the identity on its diagonal; all entries are independent otherwise.
All inputs are finite; a program needn't handle non-finite values.
Results may differ from a plain program's by a relative error of at most 0.015.
Values may be sent and summed in bfloat16 or wider, within the bound.
No kernel may reach another device: no remote copies, remote signals or barrier semaphores. Data moves between devices by JAX's collectives and lax.ppermute only.
A program may use at most 128 MiB of HBM per device.

v0:
```python
import math
import jax
import jax.numpy as jnp
from jax import lax
from jax.sharding import PartitionSpec as P

NT = 4096


def make_table(count, offset_bin):
    freq_index = jnp.arange(count, dtype=jnp.int32)
    sample = jnp.arange(NT, dtype=jnp.int32)
    phase_step = (freq_index[:, None] + offset_bin) * sample[None, :] % NT
    angles = phase_step.astype(jnp.float32) * (2.0 * math.pi / NT)
    return jnp.stack([jnp.cos(angles), -jnp.sin(angles)], axis=0).astype(jnp.bfloat16)


def shards(excitation, coupling, wavenumber, mode_counts, seg_steps, shapes, spectrum):
    sources, _, bins_here, modes_here = excitation.shape
    all_modes = coupling.shape[-1]
    columns = sources * 2 * bins_here
    first_mode = lax.axis_index("mode") * modes_here
    mode_number = first_mode + jnp.arange(modes_here, dtype=jnp.int32)
    living = (mode_number[None, :] < mode_counts[:, None]).astype(jnp.float32)
    amplitude = (
        (excitation.astype(jnp.float32) * living).astype(jnp.bfloat16).reshape(columns, modes_here)
    )
    for segment in range(coupling.shape[0]):
        stacked = coupling[segment, 0].reshape(2 * modes_here, all_modes)

        def add_portion(running, portion, offset, stacked=stacked):
            return lax.dot_general(
                portion, stacked, (((1,), (1,)), ((), ())), preferred_element_type=jnp.float32
            )

        product = add_portion(
            jnp.zeros((columns, 2 * modes_here), jnp.float32),
            lax.all_gather(amplitude, "mode", axis=1, tiled=True),
            jnp.int32(0),
        )
        product = product.reshape(sources, 2, bins_here, 2, modes_here)
        coupled_real = product[:, 0, :, 0] - product[:, 1, :, 1]
        coupled_imaginary = product[:, 1, :, 0] + product[:, 0, :, 1]
        angles = wavenumber * seg_steps[segment].astype(jnp.float32)
        factor_real = living * jnp.cos(angles)
        factor_imaginary = living * jnp.sin(angles)
        amplitude = jnp.stack(
            [
                coupled_real * factor_real - coupled_imaginary * factor_imaginary,
                coupled_real * factor_imaginary + coupled_imaginary * factor_real,
            ],
            axis=1,
        )
        amplitude = amplitude.astype(jnp.bfloat16).reshape(columns, modes_here)
    mode_shapes = shapes[0]
    field = lax.dot_general(
        lax.all_to_all(
            amplitude.reshape(sources, 2, bins_here, modes_here),
            "mode",
            split_axis=0,
            concat_axis=3,
            tiled=True,
        ),
        mode_shapes,
        (((3,), (0,)), ((), ())),
        preferred_element_type=jnp.float32,
    )
    weight_real = spectrum[0][None, :, None]
    weight_imaginary = spectrum[1][None, :, None]
    weighted = jnp.stack(
        [
            weight_real * field[:, 0] - weight_imaginary * field[:, 1],
            weight_real * field[:, 1] + weight_imaginary * field[:, 0],
        ],
        axis=1,
    ).astype(jnp.bfloat16)
    all_bins = bins_here * lax.axis_size("freq")
    offset_bin = all_bins // 16
    table = make_table(all_bins, offset_bin)
    summed = lax.dot_general(
        lax.all_to_all(weighted, "freq", split_axis=3, concat_axis=2, tiled=True),
        table,
        (((1, 2), (0, 1)), ((), ())),
        preferred_element_type=jnp.float32,
    )
    return summed * (1.0 / math.sqrt(all_bins))


def solution(mesh):
    in_specs = (
        P(None, None, "freq", "mode"),
        P(None, "freq", None, "mode", None),
        P("freq", "mode"),
        P("freq"),
        P(),
        P("freq", None, None),
        P(None, "freq"),
    )
    out_specs = P("mode", "freq", None)
    return jax.shard_map(shards, mesh=mesh, in_specs=in_specs, out_specs=out_specs, check_vma=False)
```

profile of v0, /device:TPU:1, one launch (start us, length us, event | category | flops | bytes accessed | tf_op | source)
XLA Modules:
  0.0 331.4 jit_solution(11354796678249846747)
XLA Ops:
  6.5 0.0 copy-start
  6.5 0.0 all-gather.4.cloned.1.call-start
  6.5 0.9 compare_convert_fusion
  7.4 2.0 multiply_convert_fusion
  9.4 0.0 all-gather.4.cloned.1.call-update
  9.4 0.0 all-gather.6.cloned.1.call-start
  9.5 1.4 fusion.30
  12.9 1.1 compare_select_fusion.5
  14.0 58.2 %all-gather.4.cloned.1.call-done = bf16[1024,2048]{1,0:T(8,128)(2,1)} async-done(((bf16[1024,256]{1,0:T(8,128)(2,1)}), bf16[1024,2048]{1,0:T(8,128)(2,1)}) %all-gather.4.cloned.1.call-update) | async-done | bytes 4194320 | tf_op jit(solution)/shard_map/all_gather | solution.py:38
  72.1 5.2 %fusion.15 = f32[16,2,32,2,256]{4,2,3,1,0:T(8,128)S(1)} fusion(bf16[16,2,32,2048,1]{3,2,4,1,0:T(8,128)(2,1)} %bitcast.183, bf16[3,1,2,256,2048]{4,3,2,1,0:T(8,128)(2,1)} %param.8), kind=kOutput, calls=%fused_computation.21 | convolution fusion | flops 2147483648 | bytes 8388608 | tf_op jit(solution)/shard_map/dot_general | solution.py:32
  77.4 0.3 subtract_convert_fusion.2
  77.7 0.1 pad_maximum_fusion
  77.7 0.8 copy.29
  78.6 0.0 all-gather.6.cloned.1.call-update
  78.6 0.0 all-gather.8.cloned.1.call-start
  78.6 61.2 %all-gather.6.cloned.1.call-done = bf16[1024,2048]{1,0:T(8,128)(2,1)} async-done(((bf16[1024,256]{1,0:T(8,128)(2,1)}), bf16[1024,2048]{1,0:T(8,128)(2,1)}) %all-gather.6.cloned.1.call-update) | async-done | bytes 4194320 | tf_op jit(solution)/shard_map/all_gather | solution.py:38
  139.9 5.2 %fusion.13 = f32[16,2,32,2,256]{4,2,3,1,0:T(8,128)S(1)} fusion(bf16[16,2,32,2048,1]{3,2,4,1,0:T(8,128)(2,1)} %bitcast.184, bf16[3,1,2,256,2048]{4,3,2,1,0:T(8,128)(2,1)} %param.8), kind=kOutput, calls=%fused_computation.19 | convolution fusion | flops 2147483648 | bytes 8388608 | tf_op jit(solution)/shard_map/dot_general | solution.py:32
  145.1 0.3 subtract_convert_fusion.1
  145.4 0.1 pad_maximum_fusion.1
  145.4 0.8 copy.32
  146.3 0.0 all-gather.8.cloned.1.call-update
  146.3 61.3 %all-gather.8.cloned.1.call-done = bf16[1024,2048]{1,0:T(8,128)(2,1)} async-done(((bf16[1024,256]{1,0:T(8,128)(2,1)}), bf16[1024,2048]{1,0:T(8,128)(2,1)}) %all-gather.8.cloned.1.call-update) | async-done | bytes 4194320 | tf_op jit(solution)/shard_map/all_gather | solution.py:38
  207.6 0.0 copy-start.1
  207.6 5.2 %fusion.11 = f32[16,2,32,2,256]{4,2,3,1,0:T(8,128)S(1)} fusion(bf16[16,2,32,2048,1]{3,2,4,1,0:T(8,128)(2,1)} %bitcast.185, bf16[3,1,2,256,2048]{4,3,2,1,0:T(8,128)(2,1)} %param.8), kind=kOutput, calls=%fused_computation.17 | convolution fusion | flops 2147483648 | bytes 8388608 | tf_op jit(solution)/shard_map/dot_general | solution.py:32
  212.8 0.3 subtract_convert_fusion
  213.1 0.1 pad_maximum_fusion.2
  213.1 0.8 copy.35
  214.0 3.5 %all-to-all-start = ((bf16[16,2,32,256]{3,2,1,0:T(8,128)(2,1)}), bf16[16,2,32,256]{3,2,1,0:T(8,128)(2,1)S(1)}, u32[]{:S(2)}, u32[]{:S(2)}) async-start(bf16[16,2,32,256]{3,2,1,0:T(8,128)(2,1)} %copy.35), calls=%async_computation | async-start | bytes 1048576 | tf_op jit(solution)/shard_map/all_to_all | solution.py:57
  217.5 0.0 copy-done.1
  217.5 12.2 %all-to-all-done = bf16[16,2,32,256]{3,2,1,0:T(8,128)(2,1)S(1)} async-done(((bf16[16,2,32,256]{3,2,1,0:T(8,128)(2,1)}), bf16[16,2,32,256]{3,2,1,0:T(8,128)(2,1)S(1)}, u32[]{:S(2)}, u32[]{:S(2)}) %all-to-all-start) | async-done | bytes 524320 | tf_op jit(solution)/shard_map/all_to_all | solution.py:57
  229.7 0.3 copy.55
  230.0 0.2 all_to_all.29
  230.3 0.0 copy-done
  230.3 0.5 fusion.9
  230.7 0.1 subtract_convert_fusion.3
  230.9 0.4 copy.37
  231.3 1.2 reshape.388
  232.5 13.2 %all-to-all-start.1 = ((bf16[32,2,1024]{2,1,0:T(2,128)(2,1)}), bf16[32,2,1024]{2,1,0:T(2,128)(2,1)S(1)}, u32[]{:S(2)}, u32[]{:S(2)}) async-start(bf16[32,2,1024]{2,1,0:T(2,128)(2,1)} %reshape.388), calls=%async_computation.1 | async-start | bytes 262144 | tf_op jit(solution)/shard_map/all_to_all | solution.py:81
  245.7 70.0 %cosine_convert_fusion = (bf16[1,1024,4096]{2,1,0:T(8,128)(2,1)}, bf16[1,1024,4096]{2,1,0:T(8,128)(2,1)}) fusion(s32[1024]{0:T(1024)S(1)} %iota_add_fusion), kind=kLoop, calls=%fused_computation.8 | loop fusion | flops 71303168 | bytes 16781312 | tf_op jit(solution)/shard_map/convert
  315.7 0.0 all-to-all-done.1
  315.7 0.3 reshape.389
  315.9 0.1 copy.38
  316.0 0.1 copy.39
  316.2 0.5 all_to_all.33
  316.7 8.2 %fusion.8 = f32[2,16,4096]{2,1,0:T(8,128)} fusion(bf16[2,2,1024,16]{2,3,1,0:T(8,128)(2,1)S(1)} %all_to_all.33, bf16[1,1024,4096]{2,1,0:T(8,128)(2,1)} %get-tuple-element.20, bf16[1,1024,4096]{2,1,0:T(8,128)(2,1)} %get-tuple-element.19), kind=kOutput, calls=%fused_computation.14 | convolution fusion | flops 545390592 | bytes 17432576 | tf_op jit(solution)/shard_map/dot_general | solution.py:80
  (4 shorter events, 0.0 us)
Async XLA Ops:
  6.5 223.7 %copy-start = (bf16[1,2048,512]{2,1,0:T(8,128)(2,1)S(1)}, bf16[1,2048,512]{2,1,0:T(8,128)(2,1)}, u32[]{:S(2)}) copy-start(bf16[1,2048,512]{2,1,0:T(8,128)(2,1)} %param.12) | copy-start | bytes 6291460
  6.5 65.6 %all-gather.4.cloned.1.call-start = ((), (), s32[]{:S(2)}) async-start(), calls=%async_computation.2 | async-start | bytes 4718592 | tf_op jit(solution)/shard_map/all_gather | solution.py:38
  9.4 130.5 %all-gather.6.cloned.1.call-start = ((), (), s32[]{:S(2)}) async-start(), calls=%async_computation.3 | async-start | bytes 4718592 | tf_op jit(solution)/shard_map/all_gather | solution.py:38
  78.6 129.0 %all-gather.8.cloned.1.call-start = ((), (), s32[]{:S(2)}) async-start(), calls=%async_computation.4 | async-start | bytes 4718592 | tf_op jit(solution)/shard_map/all_gather | solution.py:38
  207.6 9.9 %copy-start.1 = (f32[2,32]{1,0:T(2,128)S(1)}, f32[2,32]{1,0:T(2,128)}, u32[]{:S(2)}) copy-start(f32[2,32]{1,0:T(2,128)} %param.13) | copy-start | bytes 772
  214.0 15.7 %all-to-all-start = ((bf16[16,2,32,256]{3,2,1,0:T(8,128)(2,1)}), bf16[16,2,32,256]{3,2,1,0:T(8,128)(2,1)S(1)}, u32[]{:S(2)}, u32[]{:S(2)}) async-start(bf16[16,2,32,256]{3,2,1,0:T(8,128)(2,1)} %copy.35), calls=%async_computation | async-start | bytes 1048576 | tf_op jit(solution)/shard_map/all_to_all | solution.py:57
  232.5 83.2 %all-to-all-start.1 = ((bf16[32,2,1024]{2,1,0:T(2,128)(2,1)}), bf16[32,2,1024]{2,1,0:T(2,128)(2,1)S(1)}, u32[]{:S(2)}, u32[]{:S(2)}) async-start(bf16[32,2,1024]{2,1,0:T(2,128)(2,1)} %reshape.388), calls=%async_computation.1 | async-start | bytes 262144 | tf_op jit(solution)/shard_map/all_to_all | solution.py:81
Sparse Core Ops, SparseCore 0:
  9.5 62.5 all-gather.3
  78.7 61.1 all-gather.5
  146.4 61.1 all-gather.7
where the time goes:
time: 332 us; the launch traced here: 331 us
  waiting for transfers between devices  193 us (58%)
  other arithmetic  75.1 us (23%)
  matrix products  24.4 us (7%)
  starting transfers between devices  16.8 us (5%)
  between operations  15.3 us (5%)
  local copies, waits for them, and re-layouts  7.04 us (2%)
    all_gather x3, waiting for transfers between devices, shards(): lax.all_gather(amplitude, 'mode', axis=1, tiled=True)  181 us
    another operation x5, other arithmetic  70.9 us
    dot_general x3, matrix products, add_portion(): lax.dot_general(portion, stacked, (((1,), (1,)), ((), ())), preferred_ele...  15.7 us
    all_to_all x1, starting transfers between devices, shards(): lax.all_to_all(weighted, 'freq', split_axis=3, concat_axis=2, tiled=True)  13.2 us
    all_to_all x1, waiting for transfers between devices, shards(): lax.all_to_all(amplitude.reshape(sources, 2, bins_here, modes_here), 'mod...  12.2 us
    dot_general x1, matrix products, shards(): lax.dot_general(lax.all_to_all(weighted, 'freq', split_axis=3, concat_axi...  8.21 us
  transfers between devices with their start and end apart: 5, of which 4 were waited for; matrix products, arithmetic and copies ran while one was open for 22% of the time, Pallas kernels for 0%

commit v1 on v0

--- a/solution.py
+++ b/solution.py
@@ -3,8 +3,16 @@
 import jax.numpy as jnp
 from jax import lax
 from jax.sharding import PartitionSpec as P
+from jax.lax import all_to_all, axis_size
 
 NT = 4096
+
+
+def spots_see(bus_axis, field_in):
+    tile_out = tuple((field_in for _ in range(axis_size(bus_axis))))
+    met_up = all_to_all(jnp.stack(tile_out, axis=0), bus_axis, 0, 0)
+    b_now = jnp.concatenate(met_up, axis=1)
+    return b_now
 
 
 def make_table(count, offset_bin):
@@ -35,7 +43,7 @@
 
         product = add_portion(
             jnp.zeros((columns, 2 * modes_here), jnp.float32),
-            lax.all_gather(amplitude, "mode", axis=1, tiled=True),
+            spots_see("mode", amplitude),
             jnp.int32(0),
         )
         product = product.reshape(sources, 2, bins_here, 2, modes_here)

time: 332 us -> 473 us (1.42)
  blocking collectives: 0 us -> 196 us
  waiting for transfers between devices: 193 us -> 109 us
  local copies, waits for them, and re-layouts: 7.04 us -> 45.1 us
  between operations: 15.3 us -> 2.18 us
  starting transfers between devices: 16.8 us -> 22 us
    all_to_all x0 -> x2, blocking collectives: none -> 196 us  [spots_see(): met_up = all_to_all(jnp.stack(tile_out, axis=0), bus_axis, 0, 0)]
    all_gather x3 -> x0, waiting for transfers between devices: 181 us -> none  [shards(): lax.all_gather(amplitude, 'mode', axis=1, tiled=True)]
    all_to_all x0 -> x1, waiting for transfers between devices: none -> 93.9 us  [spots_see(): met_up = all_to_all(jnp.stack(tile_out, axis=0), bus_axis, 0, 0)]
    dot_general x0 -> x3, local copies, waits for them, and re-layouts: none -> 22.3 us  [add_portion(): lax.dot_general(portion, stacked, (((1,), (1,)), ((), ())), preferred_ele...]
    reshape x0 -> x3, local copies, waits for them, and re-layouts: none -> 15.3 us  [spots_see(): b_now = jnp.concatenate(met_up, axis=1)]
    all_to_all x0 -> x1, starting transfers between devices: none -> 9.13 us  [spots_see(): met_up = all_to_all(jnp.stack(tile_out, axis=0), bus_axis, 0, 0)]
  transfers between devices with their start and end apart: 5 -> 3, of which waited for: 4 -> 2; matrix products, arithmetic and copies ran while one was open for 22% -> 15% of each run, Pallas kernels for 0% -> 0%
where the time goes in v1:
time: 473 us; the launch traced here: 472 us
  blocking collectives  196 us (41%)
  waiting for transfers between devices  109 us (23%)
  other arithmetic  73.5 us (16%)
  local copies, waits for them, and re-layouts  45.1 us (10%)
  matrix products  24.3 us (5%)
  starting transfers between devices  22 us (5%)
    all_to_all x2, blocking collectives, spots_see(): met_up = all_to_all(jnp.stack(tile_out, axis=0), bus_axis, 0, 0)  196 us
    all_to_all x1, waiting for transfers between devices, spots_see(): met_up = all_to_all(jnp.stack(tile_out, axis=0), bus_axis, 0, 0)  93.9 us
    another operation x5, other arithmetic  70.9 us
    dot_general x3, local copies, waits for them, and re-layouts, add_portion(): lax.dot_general(portion, stacked, (((1,), (1,)), ((), ())), preferred_ele...  22.3 us
    dot_general x3, matrix products, add_portion(): lax.dot_general(portion, stacked, (((1,), (1,)), ((), ())), preferred_ele...  15.7 us
    reshape x3, local copies, waits for them, and re-layouts, spots_see(): b_now = jnp.concatenate(met_up, axis=1)  15.3 us
    all_to_all x1, waiting for transfers between devices, shards(): lax.all_to_all(amplitude.reshape(sources, 2, bins_here, modes_here), 'mod...  15.3 us
  transfers between devices with their start and end apart: 3, of which 2 were waited for; matrix products, arithmetic and copies ran while one was open for 15% of the time, Pallas kernels for 0%

profile of v1, /device:TPU:1, one launch (start us, length us, event | category | flops | bytes accessed | tf_op | source)
XLA Modules:
  0.0 472.1 jit_solution(10030179837268180067)
XLA Ops:
  0.0 0.0 copy-start
  0.0 0.9 compare_convert_fusion
  0.9 1.2 multiply_convert_fusion
  2.0 2.3 stack.39
  4.3 0.0 copy-start.2
  4.3 0.0 copy-start.1
  4.3 0.0 copy-start.3
  4.3 9.1 %all-to-all-start = ((bf16[8,1024,256]{2,1,0:T(8,128)(2,1)}), bf16[8,1024,256]{2,1,0:T(8,128)(2,1)}, u32[]{:S(2)}, u32[]{:S(2)}) async-start(bf16[8,1024,256]{2,1,0:T(8,128)(2,1)} %stack.39), calls=%async_computation | async-start | bytes 8388608 | tf_op jit(solution)/shard_map/all_to_all | solution.py:13
  13.5 0.0 copy-done.2
  13.5 0.7 fusion.33
  16.0 0.0 copy-done.1
  16.0 0.0 copy-done.3
  16.0 0.4 compare_select_fusion.5
  16.4 93.9 %all-to-all-done = bf16[8,1024,256]{2,1,0:T(8,128)(2,1)} async-done(((bf16[8,1024,256]{2,1,0:T(8,128)(2,1)}), bf16[8,1024,256]{2,1,0:T(8,128)(2,1)}, u32[]{:S(2)}, u32[]{:S(2)}) %all-to-all-start) | async-done | bytes 4194336 | tf_op jit(solution)/shard_map/all_to_all | solution.py:13
  110.3 6.5 %copy.27 = bf16[1024,8,256]{2,1,0:T(8,128)(2,1)} copy(bf16[1024,8,256]{2,0,1:T(8,128)(2,1)} %bitcast.2) | data formatting | bytes 8388608 | tf_op jit(solution)/shard_map/reshape | solution.py:14
  116.8 7.4 %reshape.397 = bf16[16,2,32,2048,1]{3,2,1,0,4:T(8,128)(2,1)} reshape(bf16[1024,8,256]{2,1,0:T(8,128)(2,1)} %copy.27) | data formatting | bytes 8388608 | tf_op jit(solution)/shard_map/dot_general | solution.py:40
  124.2 5.2 %fusion.13 = f32[16,2,32,2,256]{4,2,3,1,0:T(8,128)S(1)} fusion(bf16[16,2,32,2048,1]{3,2,1,0,4:T(8,128)(2,1)} %reshape.397, bf16[3,1,2,256,2048]{4,3,2,1,0:T(8,128)(2,1)} %param.8), kind=kOutput, calls=%fused_computation.19 | convolution fusion | flops 2147483648 | bytes 8388608 | tf_op jit(solution)/shard_map/dot_general | solution.py:40
  129.5 0.3 subtract_convert_fusion.2
  129.8 0.1 pad_maximum_fusion
  129.9 0.3 stack.41
  130.1 98.6 %all_to_all.51 = bf16[8,1024,256]{2,1,0:T(8,128)(2,1)S(1)} all-to-all(bf16[8,1024,256]{2,1,0:T(8,128)(2,1)S(1)} %stack.41), channel_id=1, replica_groups=mesh['freq'=32,'mode'=8] {'mode'}, dimensions={0} | all-to-all | bytes 8388608 | tf_op jit(solution)/shard_map/all_to_all | solution.py:13
  228.7 4.4 copy.31
  233.1 7.5 %reshape.399 = bf16[16,2,32,2048,1]{3,2,1,0,4:T(8,128)(2,1)} reshape(bf16[1024,8,256]{2,1,0:T(8,128)(2,1)} %copy.31) | data formatting | bytes 8388608 | tf_op jit(solution)/shard_map/dot_general | solution.py:40
  240.6 5.2 %fusion.11 = f32[16,2,32,2,256]{4,2,3,1,0:T(8,128)S(1)} fusion(bf16[16,2,32,2048,1]{3,2,1,0,4:T(8,128)(2,1)} %reshape.399, bf16[3,1,2,256,2048]{4,3,2,1,0:T(8,128)(2,1)} %param.8), kind=kOutput, calls=%fused_computation.17 | convolution fusion | flops 2147483648 | bytes 8388608 | tf_op jit(solution)/shard_map/dot_general | solution.py:40
  245.8 0.3 subtract_convert_fusion.1
  246.1 0.1 pad_maximum_fusion.1
  246.2 0.3 stack.43
  246.5 97.3 %all_to_all.52 = bf16[8,1024,256]{2,1,0:T(8,128)(2,1)S(1)} all-to-all(bf16[8,1024,256]{2,1,0:T(8,128)(2,1)S(1)} %stack.43), channel_id=1, replica_groups=mesh['freq'=32,'mode'=8] {'mode'}, dimensions={0} | all-to-all | bytes 8388608 | tf_op jit(solution)/shard_map/all_to_all | solution.py:13
  343.7 4.4 copy.35
  348.1 7.5 %reshape.401 = bf16[16,2,32,2048,1]{3,2,1,0,4:T(8,128)(2,1)} reshape(bf16[1024,8,256]{2,1,0:T(8,128)(2,1)} %copy.35) | data formatting | bytes 8388608 | tf_op jit(solution)/shard_map/dot_general | solution.py:40
  355.5 5.2 %fusion.9 = f32[16,2,32,2,256]{4,2,3,1,0:T(8,128)S(1)} fusion(bf16[16,2,32,2048,1]{3,2,1,0,4:T(8,128)(2,1)} %reshape.401, bf16[3,1,2,256,2048]{4,3,2,1,0:T(8,128)(2,1)} %param.8), kind=kOutput, calls=%fused_computation.15 | convolution fusion | flops 2147483648 | bytes 8388608 | tf_op jit(solution)/shard_map/dot_general | solution.py:40
  360.8 0.0 copy-start.4
  360.8 0.3 subtract_convert_fusion
  361.1 0.1 pad_maximum_fusion.2
  361.1 0.8 copy.38
  362.0 3.7 all-to-all-start.3
  365.7 0.0 copy-done.4
  365.7 15.3 %all-to-all-done.3 = bf16[16,2,32,256]{3,2,1,0:T(8,128)(2,1)S(1)} async-done(((bf16[16,2,32,256]{3,2,1,0:T(8,128)(2,1)}), bf16[16,2,32,256]{3,2,1,0:T(8,128)(2,1)S(1)}, u32[]{:S(2)}, u32[]{:S(2)}) %all-to-all-start.3) | async-done | bytes 524320 | tf_op jit(solution)/shard_map/all_to_all | solution.py:65
  381.0 0.3 copy.58
  381.3 0.2 all_to_all.41
  381.6 0.0 copy-done
  381.6 0.4 fusion.15
  382.0 0.1 subtract_convert_fusion.3
  382.2 0.4 copy.40
  382.5 1.2 reshape.409
  383.7 9.1 %all-to-all-start.4 = ((bf16[32,2,1024]{2,1,0:T(2,128)(2,1)}), bf16[32,2,1024]{2,1,0:T(2,128)(2,1)S(1)}, u32[]{:S(2)}, u32[]{:S(2)}) async-start(bf16[32,2,1024]{2,1,0:T(2,128)(2,1)} %reshape.409), calls=%async_computation.4 | async-start | bytes 262144 | tf_op jit(solution)/shard_map/all_to_all | solution.py:89
  392.9 70.0 %cosine_convert_fusion = (bf16[1,1024,4096]{2,1,0:T(8,128)(2,1)}, bf16[1,1024,4096]{2,1,0:T(8,128)(2,1)}) fusion(s32[1024]{0:T(1024)S(1)} %iota_add_fusion), kind=kLoop, calls=%fused_computation.8 | loop fusion | flops 71303168 | bytes 16781312 | tf_op jit(solution)/shard_map/convert
  462.9 0.0 all-to-all-done.4
  462.9 0.3 reshape.410
  463.2 0.1 copy.41
  463.2 0.1 copy.42
  463.4 0.5 all_to_all.45
  463.9 8.2 %fusion.8 = f32[2,16,4096]{2,1,0:T(8,128)} fusion(bf16[2,2,1024,16]{2,3,1,0:T(8,128)(2,1)S(1)} %all_to_all.45, bf16[1,1024,4096]{2,1,0:T(8,128)(2,1)} %get-tuple-element.20, bf16[1,1024,4096]{2,1,0:T(8,128)(2,1)} %get-tuple-element.19), kind=kOutput, calls=%fused_computation.14 | convolution fusion | flops 545390592 | bytes 17432576 | tf_op jit(solution)/shard_map/dot_general | solution.py:88
  (6 shorter events, 0.1 us)
Async XLA Ops:
  0.0 381.6 %copy-start = (bf16[1,2048,512]{2,1,0:T(8,128)(2,1)S(1)}, bf16[1,2048,512]{2,1,0:T(8,128)(2,1)}, u32[]{:S(2)}) copy-start(bf16[1,2048,512]{2,1,0:T(8,128)(2,1)} %param.12) | copy-start | bytes 6291460
  4.3 9.1 %copy-start.2 = (s32[3]{0:T(128)S(1)}, s32[3]{0:T(128)}, u32[]{:S(2)}) copy-start(s32[3]{0:T(128)} %param.11) | copy-start | bytes 40
  4.3 11.7 %copy-start.1 = (f32[32,256]{1,0:T(8,128)S(1)}, f32[32,256]{1,0:T(8,128)}, u32[]{:S(2)}) copy-start(f32[32,256]{1,0:T(8,128)} %param.9) | copy-start | bytes 98308
  4.3 11.7 %copy-start.3 = (s32[32]{0:T(128)S(1)}, s32[32]{0:T(128)}, u32[]{:S(2)}) copy-start(s32[32]{0:T(128)} %param.10) | copy-start | bytes 388
  4.3 106.0 %all-to-all-start = ((bf16[8,1024,256]{2,1,0:T(8,128)(2,1)}), bf16[8,1024,256]{2,1,0:T(8,128)(2,1)}, u32[]{:S(2)}, u32[]{:S(2)}) async-start(bf16[8,1024,256]{2,1,0:T(8,128)(2,1)} %stack.39), calls=%async_computation | async-start | bytes 8388608 | tf_op jit(solution)/shard_map/all_to_all | solution.py:13
  360.8 4.9 %copy-start.4 = (f32[2,32]{1,0:T(2,128)S(1)}, f32[2,32]{1,0:T(2,128)}, u32[]{:S(2)}) copy-start(f32[2,32]{1,0:T(2,128)} %param.13) | copy-start | bytes 772
  362.0 19.0 %all-to-all-start.3 = ((bf16[16,2,32,256]{3,2,1,0:T(8,128)(2,1)}), bf16[16,2,32,256]{3,2,1,0:T(8,128)(2,1)S(1)}, u32[]{:S(2)}, u32[]{:S(2)}) async-start(bf16[16,2,32,256]{3,2,1,0:T(8,128)(2,1)} %copy.38), calls=%async_computation.3 | async-start | bytes 1048576 | tf_op jit(solution)/shard_map/all_to_all | solution.py:65
  383.7 79.2 %all-to-all-start.4 = ((bf16[32,2,1024]{2,1,0:T(2,128)(2,1)}), bf16[32,2,1024]{2,1,0:T(2,128)(2,1)S(1)}, u32[]{:S(2)}, u32[]{:S(2)}) async-start(bf16[32,2,1024]{2,1,0:T(2,128)(2,1)} %reshape.409), calls=%async_computation.4 | async-start | bytes 262144 | tf_op jit(solution)/shard_map/all_to_all | solution.py:89
